TPU v7x, 256 devices: a whole 4x4x8 slice. The times are simulated.
256 devices in a mesh: dp: 16 (over x, y), tensor: 16 (over z, core).
Axes of the slice: x: 4, y: 4, z: 8, core: 2. Of those that a mesh axis runs over, the one named last changes fastest.
Arguments:
- tokens: bfloat16 [32768, 1280], P(('dp', 'tensor'))
- cotangent: bfloat16 [32768, 1280], P(('dp', 'tensor')), may hold values from -6 to 6
- gate_weights: float32 [32768, 2], P(('dp', 'tensor')), may hold values from 0.2 to 1
- routes: int32 [32768, 2], P(('dp', 'tensor')), may hold values from 0 to 31, as said below
- slot_index: int32 [32768, 2], P(('dp', 'tensor')), may hold values from -1 to 1, as said below
- qkv_weight: bfloat16 [1280, 16, 240], P(None, 'tensor'), may hold values from -0.15625 to 0.15625
- proj_weight: bfloat16 [16, 80, 1280], P('tensor'), may hold values from -1.25 to 1.25
- up_weight: bfloat16 [32, 1280, 5120], P('dp', None, 'tensor'), may hold values from -0.15625 to 0.15625
- down_weight: bfloat16 [32, 5120, 1280], P('dp', 'tensor'), may hold values from -0.078125 to 0.078125
Outputs:
- layer_out: bfloat16 [32768, 1280], P(('dp', 'tensor'))
- gate_grad: float32 [32768, 2], P(('dp', 'tensor'))
- grad_qkv: float32 [1280, 16, 240], P('dp', 'tensor')
- grad_proj: float32 [16, 80, 1280], P('tensor', None, 'dp')
- grad_up: bfloat16 [32, 1280, 5120], P('dp', None, 'tensor')
- grad_down: bfloat16 [32, 5120, 1280], P('dp', 'tensor')
Inputs may be any that keep to these rules, and one draw needn't show every extreme that they name: `routes`: the two experts of a row differ. `slot_index`: -1 marks a dropped pair; within the rows of one device (aligned blocks of 128 rows) and one expert, the kept pairs hold the slots 0, 1, 2, ... without gaps, each at most once.
All inputs are finite; a program needn't handle non-finite values.
Results may differ from a plain program's by a relative error of at most 0.035.
Values may be sent and summed in bfloat16 or wider, within the bound.
A program may use at most 128 MiB of HBM per device.

v0:
```python
from functools import partial
import math
import jax
import jax.numpy as jnp
from jax import lax
from jax.sharding import PartitionSpec as P

CAP = 2
epsilon = 1e-06
half_root = 1.0 / math.sqrt(2.0)
bell_scale = 1.0 / math.sqrt(2.0 * math.pi)


def norm_parts(row_block):
    widened = row_block.astype(jnp.float32)
    center = widened - jnp.mean(widened, axis=-1, keepdims=True)
    factor = lax.rsqrt(jnp.mean(center * center, axis=-1, keepdims=True) + epsilon)
    return (center * factor, factor)


def norm_back(normal_rows, factor, upstream):
    mean_up = jnp.mean(upstream, axis=-1, keepdims=True)
    mean_mix = jnp.mean(upstream * normal_rows, axis=-1, keepdims=True)
    return factor * (upstream - mean_up - normal_rows * mean_mix)


def gelu_value(pre_act):
    return 0.5 * pre_act * (1.0 + lax.erf(pre_act * half_root))


def gelu_slope(pre_act):
    return (
        0.5 * (1.0 + lax.erf(pre_act * half_root))
        + pre_act * jnp.exp(-0.5 * pre_act * pre_act) * bell_scale
    )


def block_shares(query_block, key_rows, score_scale):
    scores = (
        jnp.einsum("qk,tk->qt", query_block, key_rows, preferred_element_type=jnp.float32)
        * score_scale
    )
    raised = jnp.exp(scores)
    return raised / jnp.sum(raised, axis=-1, keepdims=True)


def attend_head(queries, key_rows, value_rows, block_rows, score_scale):
    block_count = queries.shape[0] // block_rows

    def attend_one_block(query_block):
        shares = block_shares(query_block, key_rows, score_scale)
        context = jnp.dot(
            shares.astype(jnp.bfloat16), value_rows, preferred_element_type=jnp.float32
        )
        return context.astype(jnp.bfloat16)

    outputs = lax.map(attend_one_block, queries.reshape(block_count, block_rows, queries.shape[1]))
    return outputs.reshape(queries.shape)


def head_backward(queries, key_rows, value_rows, grad_context, block_rows, score_scale):
    block_count = queries.shape[0] // block_rows

    def head_one_block(carry, pieces):
        grad_keys, grad_values = carry
        query_block, grad_block = pieces
        shares = block_shares(query_block, key_rows, score_scale)
        grad_shares = jnp.einsum(
            "qk,tk->qt", grad_block, value_rows, preferred_element_type=jnp.float32
        )
        grad_scores = (
            shares
            * (grad_shares - jnp.sum(shares * grad_shares, axis=-1, keepdims=True))
            * score_scale
        ).astype(jnp.bfloat16)
        grad_query = jnp.dot(grad_scores, key_rows, preferred_element_type=jnp.float32).astype(
            jnp.bfloat16
        )
        grad_keys = grad_keys + jnp.einsum(
            "qt,qk->tk", grad_scores, query_block, preferred_element_type=jnp.float32
        )
        grad_values = grad_values + jnp.einsum(
            "qt,qk->tk", shares.astype(jnp.bfloat16), grad_block, preferred_element_type=jnp.float32
        )
        return ((grad_keys, grad_values), grad_query)

    zeros_rows = jnp.zeros(key_rows.shape, jnp.float32)
    shaped = (
        queries.reshape(block_count, block_rows, queries.shape[1]),
        grad_context.reshape(block_count, block_rows, queries.shape[1]),
    )
    (grad_keys, grad_values), grad_queries = lax.scan(
        head_one_block, (zeros_rows, zeros_rows), shaped
    )
    return (
        grad_queries.reshape(queries.shape),
        grad_keys.astype(jnp.bfloat16),
        grad_values.astype(jnp.bfloat16),
    )


def return_slots(expert_partial):
    summed = lax.psum_scatter(
        expert_partial.astype(jnp.bfloat16), "tensor", scatter_dimension=0, tiled=True
    ).astype(jnp.float32)
    returned = lax.all_to_all(
        summed[0].astype(jnp.bfloat16), "dp", split_axis=0, concat_axis=0, tiled=True
    )
    return returned.reshape(
        returned.shape[0] * returned.shape[1] * returned.shape[2], returned.shape[3]
    )


def shards(
    tokens,
    cotangent,
    gate_weights,
    routes,
    slot_index,
    qkv_weight,
    proj_weight,
    up_weight,
    down_weight,
):
    rows_dev, model_width = tokens.shape
    head_size = qkv_weight.shape[2] // 3
    score_scale = head_size ** (-0.5)
    group_count = lax.axis_size("dp")
    local_experts = up_weight.shape[0]
    places = group_count * local_experts * CAP
    normal_in, factor_in = norm_parts(tokens)
    normed = normal_in.astype(jnp.bfloat16)
    full_norm = lax.all_gather(normed, "tensor", axis=0, tiled=True)
    seq_len = full_norm.shape[0]
    block_rows = min(512, seq_len)
    qkv_rows = jnp.einsum(
        "sd,dhc->hsc", full_norm, qkv_weight, preferred_element_type=jnp.float32
    ).astype(jnp.bfloat16)
    queries = qkv_rows[:, :, :head_size]
    key_rows = qkv_rows[:, :, head_size : 2 * head_size]
    value_rows = qkv_rows[:, :, 2 * head_size :]
    context = jax.vmap(partial(attend_head, block_rows=block_rows, score_scale=score_scale))(
        queries, key_rows, value_rows
    )
    attention = lax.psum_scatter(
        jnp.einsum("hsk,hkd->sd", context, proj_weight, preferred_element_type=jnp.float32).astype(
            jnp.bfloat16
        ),
        "tensor",
        scatter_dimension=0,
        tiled=True,
    ).astype(jnp.float32)
    mid = (tokens.astype(jnp.float32) + attention).astype(jnp.bfloat16)
    normal_mid, factor_mid = norm_parts(mid)
    mid_normed = normal_mid.astype(jnp.bfloat16)
    slot_code = jnp.where(slot_index >= 0, routes * CAP + slot_index, -1)
    positions = jnp.arange(places, dtype=jnp.int32)
    pick_both = (slot_code[None, :, :] == positions[:, None, None]).astype(jnp.bfloat16)
    pick_first = pick_both[:, :, 0]
    pick_second = pick_both[:, :, 1]
    dispatch_rows = pick_first + pick_second
    outgoing = jnp.dot(dispatch_rows, mid_normed, preferred_element_type=jnp.float32).astype(
        jnp.bfloat16
    )
    outgoing = outgoing.reshape(group_count, local_experts, CAP, model_width)
    landed = lax.all_to_all(outgoing, "dp", split_axis=0, concat_axis=0, tiled=True)
    arrived = lax.all_gather(landed[None], "tensor", axis=0, tiled=True)
    pre_act = jnp.einsum("tsecd,edf->tsecf", arrived, up_weight, preferred_element_type=jnp.float32)
    hidden = gelu_value(pre_act).astype(jnp.bfloat16)
    expert_partial = jnp.einsum(
        "tsecf,efd->tsecd", hidden, down_weight, preferred_element_type=jnp.float32
    )
    returned = return_slots(expert_partial)
    expert_first = jnp.einsum("pr,pd->rd", pick_first, returned, preferred_element_type=jnp.float32)
    expert_second = jnp.einsum(
        "pr,pd->rd", pick_second, returned, preferred_element_type=jnp.float32
    )
    mixed_rows = gate_weights[:, 0:1] * expert_first + gate_weights[:, 1:2] * expert_second
    layer_out = (mid.astype(jnp.float32) + mixed_rows).astype(jnp.bfloat16)
    upstream = cotangent.astype(jnp.float32)
    gate_grad = jnp.stack(
        [jnp.sum(upstream * expert_first, axis=-1), jnp.sum(upstream * expert_second, axis=-1)],
        axis=1,
    )
    grad_first = (gate_weights[:, 0:1] * upstream).astype(jnp.bfloat16)
    grad_second = (gate_weights[:, 1:2] * upstream).astype(jnp.bfloat16)
    grad_outgoing = jnp.dot(pick_first, grad_first, preferred_element_type=jnp.float32) + jnp.dot(
        pick_second, grad_second, preferred_element_type=jnp.float32
    )
    grad_outgoing = grad_outgoing.astype(jnp.bfloat16).reshape(
        group_count, local_experts, CAP, model_width
    )
    grad_landed = lax.all_to_all(grad_outgoing, "dp", split_axis=0, concat_axis=0, tiled=True)
    grad_arrived = lax.all_gather(grad_landed[None], "tensor", axis=0, tiled=True)
    grad_hidden = jnp.einsum(
        "tsecd,efd->tsecf", grad_arrived, down_weight, preferred_element_type=jnp.float32
    )
    grad_pre = (grad_hidden * gelu_slope(pre_act)).astype(jnp.bfloat16)
    grad_down = jnp.einsum(
        "tsecf,tsecd->efd", hidden, grad_arrived, preferred_element_type=jnp.float32
    ).astype(jnp.bfloat16)
    grad_up = jnp.einsum(
        "tsecd,tsecf->edf", arrived, grad_pre, preferred_element_type=jnp.float32
    ).astype(jnp.bfloat16)
    grad_partial = jnp.einsum(
        "tsecf,edf->tsecd", grad_pre, up_weight, preferred_element_type=jnp.float32
    )
    grad_back = return_slots(grad_partial)
    grad_norm = jnp.einsum(
        "pr,pd->rd", dispatch_rows, grad_back, preferred_element_type=jnp.float32
    )
    grad_mid = (upstream + norm_back(normal_mid, factor_mid, grad_norm)).astype(jnp.bfloat16)
    full_grad = lax.all_gather(grad_mid, "tensor", axis=0, tiled=True)
    grad_context = jnp.einsum(
        "sd,hkd->hsk", full_grad, proj_weight, preferred_element_type=jnp.float32
    ).astype(jnp.bfloat16)
    grad_proj = jnp.einsum("hsk,sd->hkd", context, full_grad, preferred_element_type=jnp.float32)
    grad_queries, grad_keys, grad_values = jax.vmap(
        partial(head_backward, block_rows=block_rows, score_scale=score_scale)
    )(queries, key_rows, value_rows, grad_context)
    grad_rows = jnp.concatenate([grad_queries, grad_keys, grad_values], axis=-1)
    grad_qkv = jnp.einsum("sd,hsc->dhc", full_norm, grad_rows, preferred_element_type=jnp.float32)
    grad_qkv, grad_proj = (
        lax.psum_scatter(
            grad_qkv.astype(jnp.bfloat16), "dp", scatter_dimension=0, tiled=True
        ).astype(jnp.float32),
        lax.psum_scatter(
            grad_proj.astype(jnp.bfloat16), "dp", scatter_dimension=2, tiled=True
        ).astype(jnp.float32),
    )
    return (layer_out, gate_grad, grad_qkv, grad_proj, grad_up, grad_down)


def solution(mesh):
    return jax.shard_map(
        shards,
        mesh=mesh,
        in_specs=(
            P(("dp", "tensor"), None),
            P(("dp", "tensor"), None),
            P(("dp", "tensor"), None),
            P(("dp", "tensor"), None),
            P(("dp", "tensor"), None),
            P(None, "tensor", None),
            P("tensor", None, None),
            P("dp", None, "tensor"),
            P("dp", "tensor", None),
        ),
        out_specs=(
            P(("dp", "tensor"), None),
            P(("dp", "tensor"), None),
            P("dp", "tensor", None),
            P("tensor", None, "dp"),
            P("dp", None, "tensor"),
            P("dp", "tensor", None),
        ),
        check_vma=False,
    )
```

profile of v0, /device:TPU:2, one launch (start us, length us, event | category | flops | bytes accessed | tf_op | source)
XLA Modules:
  0.0 631.2 jit_solution(2711527637385925915)
XLA Ops:
  7.2 1.2 convert_reduce_fusion.1
  8.4 1.2 fusion.86
  9.7 1.9 fusion.87
  11.7 46.4 %all-gather.7.cloned.1.call-done = bf16[2048,1280]{1,0:T(8,128)(2,1)} async-done(((bf16[128,1280]{1,0:T(8,128)(2,1)}), bf16[2048,1280]{1,0:T(8,128)(2,1)}) %all-gather.7.cloned.1.call-update) | async-done | bytes 5242896 | tf_op jit(solution)/shard_map/all_gather | solution.py:133
  58.0 4.2 fusion.47
  62.3 1.0 copy.50
  63.9 8.0 %while.25 = (s32[]{:T(128)}, bf16[4,1,512,80]{2,3,1,0:T(8,128)(2,1)S(1)}, bf16[4,1,512,80]{3,2,1,0:T(8,128)(2,1)S(1)}, bf16[1,2048,80]{2,1,0:T(8,128)(2,1)S(1)}, bf16[1,2048,80]{2,1,0:T(8,128)(2,1)}, /*index=5*/s32[]{:T(128)}) while((s32[]{:T(128)}, bf16[4,1,512,80]{2,3,1,0:T(8,128)(2,1)S(1)}, bf16[4,1,512,80]{3,2,1,0:T(8,128)(2,1)S(1)}, ...), condition=%wide.region_4.5_spmd, body=%wide.region_2.4_spmd.sunk | while | flops 340827648 | bytes 10965105 | solution.py:57
  65.0 0.9 fusion.145
  66.0 0.8 fusion.144
  67.0 0.9 fusion.145
  69.0 0.9 fusion.145
  71.0 0.9 fusion.145
  72.3 3.9 convolution_convert_fusion.1
  77.6 62.2 %reduce-scatter.12.cloned.1.call-done = bf16[128,1280]{1,0:T(8,128)(2,1)} async-done(((bf16[2048,1280]{1,0:T(8,128)(2,1)}), bf16[128,1280]{1,0:T(8,128)(2,1)}) %reduce-scatter.12.cloned.1.call-update) | async-done | bytes 327696 | tf_op jit(solution)/shard_map/reduce_scatter | solution.py:145
  139.7 1.2 convert_reduce_fusion
  141.7 1.7 convolution_convert_fusion.8
  143.4 1.6 reshape.172
  145.1 13.8 %all_to_all.20 = bf16[16,2,2,1280]{3,2,1,0:T(2,128)(2,1)S(1)} all-to-all(bf16[16,2,2,1280]{3,2,1,0:T(2,128)(2,1)} %reshape.172), channel_id=1, replica_groups=mesh['dp'=16,'tensor'=16] {'dp'}, dimensions={0} | all-to-all | bytes 327680 | tf_op jit(solution)/shard_map/all_to_all | solution.py:166
  160.3 1.3 fusion.97
  161.7 1.7 fusion.48
  163.4 1.6 reshape.174
  165.0 11.6 %all_to_all.21 = bf16[16,2,2,1280]{3,2,1,0:T(2,128)(2,1)S(1)} all-to-all(bf16[16,2,2,1280]{3,2,1,0:T(2,128)(2,1)} %reshape.174), channel_id=1, replica_groups=mesh['dp'=16,'tensor'=16] {'dp'}, dimensions={0} | all-to-all | bytes 327680 | tf_op jit(solution)/shard_map/all_to_all | solution.py:193
  177.5 19.0 %all-gather.11.cloned.1.call-done = bf16[256,2,2,1280]{3,0,2,1:T(8,128)(2,1)} async-done(((bf16[16,2,2,1280]{3,0,2,1:T(8,128)(2,1)}), bf16[256,2,2,1280]{3,0,2,1:T(8,128)(2,1)}) %all-gather.11.cloned.1.call-update) | async-done | bytes 2621456 | tf_op jit(solution)/shard_map/all_gather | solution.py:167
  196.6 4.7 fusion.62
  201.2 36.6 %all-gather.13.cloned.1.call-done = bf16[256,2,2,1280]{3,0,2,1:T(8,128)(2,1)} async-done(((bf16[16,2,2,1280]{3,0,2,1:T(8,128)(2,1)}), bf16[256,2,2,1280]{3,0,2,1:T(8,128)(2,1)}) %all-gather.13.cloned.1.call-update) | async-done | bytes 2621456 | tf_op jit(solution)/shard_map/all_gather | solution.py:194
  237.8 4.3 fusion.60
  242.1 0.9 copy-done.10
  243.0 3.0 fusion.38
  246.0 3.0 fusion.37
  250.3 122.9 %all-reduce.9.cloned.1.call-done = (bf16[16,16,2,2,1280]{4,1,3,0,2:T(8,128)(2,1)}, bf16[16,16,2,2,1280]{4,1,3,0,2:T(8,128)(2,1)}) async-done(((bf16[16,16,2,2,1280]{4,1,3,0,2:T(8,128)(2,1)}, bf16[16,16,2,2,1280]{4,1,3,0,2:T(8,128)(2,1)}), (bf16[16,16,2,2,1280]{4,1,3,0,2:T(8,128)(2,1)}, bf16[16,16,2,2,1280]{4,1,3,0,2:T(8,128)(2,1)})) %all-reduce.9.cloned.1.call-update) | async-done | bytes 5242896
  373.2 1.6 dynamic-slice_bitcast_fusion
  375.5 7.3 %all-to-all-start.3 = ((bf16[16,2,2,1280]{3,2,1,0:T(2,128)(2,1)}), bf16[16,2,2,1280]{3,2,1,0:T(2,128)(2,1)S(1)}, u32[]{:S(2)}, u32[]{:S(2)}) async-start(bf16[16,2,2,1280]{3,2,1,0:T(2,128)(2,1)} %copy.57), calls=%async_computation.4 | async-start | bytes 327680 | tf_op jit(solution)/shard_map/all_to_all | solution.py:106
  382.8 1.6 dynamic-slice_bitcast_fusion.1
  385.2 4.1 all-to-all-done.3
  389.3 5.1 all-to-all-start.1
  394.6 1.9 fusion.114
  396.5 4.4 all-to-all-done.1
  401.3 3.0 fusion.90
  404.4 1.3 dynamic-slice.4
  406.3 4.0 fusion.40
  410.2 35.1 %all-gather.9.cloned.1.call-done = bf16[2048,1280]{1,0:T(8,128)(2,1)} async-done(((bf16[128,1280]{1,0:T(8,128)(2,1)}), bf16[2048,1280]{1,0:T(8,128)(2,1)}) %all-gather.9.cloned.1.call-update) | async-done | bytes 5242896 | tf_op jit(solution)/shard_map/all_gather | solution.py:213
  445.3 4.2 fusion.50
  449.8 4.2 fusion.49
  454.0 1.0 copy.72
  455.1 23.7 %while.26 = (s32[]{:T(128)}, f32[1,2048,80]{1,2,0:T(8,128)S(1)}, f32[1,2048,80]{1,2,0:T(8,128)S(1)}, bf16[4,1,512,80]{2,3,1,0:T(8,128)(2,1)S(1)}, bf16[4,1,512,8...) while((s32[]{:T(128)}, f32[1,2048,80]{1,2,0:T(8,128)S(1)}, ...), condition=%wide.region_17.18_spmd.clone, body=%wide.region_14.17_spmd.clone.sunk | while | flops 855284736 | bytes 37580964 | solution.py:92
  456.2 0.9 fusion.154
  457.1 1.4 multiply_reduce_fusion.2
  458.5 1.1 multiply_convert_fusion.2
  462.1 0.9 fusion.154
  463.0 1.4 multiply_reduce_fusion.2
  464.4 1.1 multiply_convert_fusion.2
  468.0 0.9 fusion.154
  468.9 1.4 multiply_reduce_fusion.2
  470.4 1.1 multiply_convert_fusion.2
  473.9 1.0 fusion.154
  474.9 1.4 multiply_reduce_fusion.2
  476.3 1.1 multiply_convert_fusion.2
  478.9 4.0 convolution_convert_fusion.4
  482.9 1.1 copy.82
  484.0 4.1 fusion.39
  488.7 52.8 %all-reduce.7.cloned.1.call-done = bf16[1,80,1280]{2,1,0:T(8,128)(2,1)} async-done(((bf16[1,80,1280]{2,1,0:T(8,128)(2,1)}), bf16[1,80,1280]{2,1,0:T(8,128)(2,1)}) %all-reduce.7.cloned.1.call-update) | async-done | bytes 204816
  541.5 1.5 dynamic-slice_convert_fusion
  543.0 79.8 %reduce-scatter.14.cloned.1.call-done = bf16[80,240]{1,0:T(8,128)(2,1)} async-done(((bf16[1280,240]{1,0:T(8,128)(2,1)}), bf16[80,240]{1,0:T(8,128)(2,1)}) %reduce-scatter.14.cloned.1.call-update) | async-done | bytes 38416
  622.7 0.9 copy.83
  (126 shorter events, 23.7 us)
Async XLA Ops:
  7.2 189.4 %copy-start = (bf16[2,1280,320]{1,2,0:T(8,128)(2,1)S(1)}, bf16[2,1280,320]{1,2,0:T(8,128)(2,1)}, u32[]{:S(2)}) copy-start(bf16[2,1280,320]{1,2,0:T(8,128)(2,1)} %param.20) | copy-start | bytes 4915204
  7.2 50.8 %all-gather.7.cloned.1.call-start = ((), (), s32[]{:S(2)}) async-start(), calls=%async_computation.6 | async-start | bytes 5570560 | tf_op jit(solution)/shard_map/all_gather | solution.py:133
  11.6 128.1 %reduce-scatter.12.cloned.1.call-start = ((), (), s32[]{:S(2)}) async-start(), calls=%async_computation.7 | async-start | bytes 5570560 | tf_op jit(solution)/shard_map/reduce_scatter | solution.py:145
  63.9 8.4 %copy-start.7 = (bf16[1,80,1280]{2,1,0:T(8,128)(2,1)S(1)}, bf16[1,80,1280]{2,1,0:T(8,128)(2,1)}, u32[]{:S(2)}) copy-start(bf16[1,80,1280]{2,1,0:T(8,128)(2,1)} %param.19) | copy-start | bytes 614404
  63.9 1.1 copy-start.13
  66.0 1.0 copy-start.13
  68.0 1.0 copy-start.13
  70.0 1.0 copy-start.13
  76.2 0.7 copy-start.19
  76.2 0.7 copy-start.20
  76.2 63.5 %copy-start.2 = (bf16[128,1280]{1,0:T(8,128)(2,1)S(1)}, bf16[128,1280]{1,0:T(8,128)(2,1)}, u32[]{:S(2)}) copy-start(bf16[128,1280]{1,0:T(8,128)(2,1)} %param.13) | copy-start | bytes 983044
  76.3 120.3 %all-gather.11.cloned.1.call-start = ((), (), s32[]{:S(2)}) async-start(), calls=%async_computation.9 | async-start | bytes 2785280 | tf_op jit(solution)/shard_map/all_gather | solution.py:167
  140.9 0.7 copy-start.3
  140.9 20.8 %copy-start.6 = (bf16[128,1280]{1,0:T(8,128)(2,1)S(1)}, bf16[128,1280]{1,0:T(8,128)(2,1)}, u32[]{:S(2)}) copy-start(bf16[128,1280]{1,0:T(8,128)(2,1)} %param.14) | copy-start | bytes 983044
  141.2 0.5 copy-start.21
  159.5 78.3 %all-gather.13.cloned.1.call-start = ((), (), s32[]{:S(2)}) async-start(), calls=%async_computation.10 | async-start | bytes 2785280 | tf_op jit(solution)/shard_map/all_gather | solution.py:194
  160.3 1.3 copy-start.17
  177.3 195.9 %all-reduce.9.cloned.1.call-start = ((), (), s32[]{:S(2)}) async-start(), calls=%async_computation.13 | async-start | bytes 10485760
  242.1 0.9 copy-start.10
  243.0 3.0 copy-start.5
  243.0 3.0 copy-start.8
  249.0 0.7 copy-start.25
  249.0 145.5 %copy-start.4 = (bf16[128,1280]{1,0:T(8,128)(2,1)S(1)}, bf16[128,1280]{1,0:T(8,128)(2,1)}, u32[]{:S(2)}) copy-start(bf16[128,1280]{1,0:T(8,128)(2,1)} %copy-done.3) | copy-start | bytes 983044
  249.0 145.5 %copy-start.22 = (f32[128]{0:T(128)S(1)}, f32[128]{0:T(128)}, u32[]{:S(2)}) copy-start(f32[128]{0:T(128)} %copy-done.21) | copy-start | bytes 1540
  249.1 151.9 %copy-start.16 = (pred[64,128,2]{1,0,2:T(32,128)(4,1)S(1)}, pred[64,128,2]{1,0,2:T(32,128)(4,1)}, u32[]{:S(2)}) copy-start(pred[64,128,2]{1,0,2:T(32,128)(4,1)} %get-tuple-element.212) | copy-start | bytes 49156
  249.1 152.2 %copy-start.18 = (f32[128]{0:T(128)S(1)}, f32[128]{0:T(128)}, u32[]{:S(2)}) copy-start(f32[128]{0:T(128)} %copy-done.17) | copy-start | bytes 1540
  375.5 13.7 %all-to-all-start.3 = ((bf16[16,2,2,1280]{3,2,1,0:T(2,128)(2,1)}), bf16[16,2,2,1280]{3,2,1,0:T(2,128)(2,1)S(1)}, u32[]{:S(2)}, u32[]{:S(2)}) async-start(bf16[16,2,2,1280]{3,2,1,0:T(2,128)(2,1)} %copy.57), calls=%async_computation.4 | async-start | bytes 327680 | tf_op jit(solution)/shard_map/all_to_all | solution.py:106
  389.3 11.6 %all-to-all-start.1 = ((bf16[16,2,2,1280]{3,2,1,0:T(2,128)(2,1)}), bf16[16,2,2,1280]{3,2,1,0:T(2,128)(2,1)S(1)}, u32[]{:S(2)}, u32[]{:S(2)}) async-start(bf16[16,2,2,1280]{3,2,1,0:T(2,128)(2,1)} %copy.54), calls=%async_computation.2 | async-start | bytes 327680 | tf_op jit(solution)/shard_map/all_to_all | solution.py:106
  394.4 50.9 %all-gather.9.cloned.1.call-start = ((), (), s32[]{:S(2)}) async-start(), calls=%async_computation.8 | async-start | bytes 5570560 | tf_op jit(solution)/shard_map/all_gather | solution.py:213
  394.6 11.7 %copy-start.11 = (bf16[16,16,2,2,320]{4,1,3,0,2:T(8,128)(2,1)S(1)}, bf16[16,16,2,2,320]{4,1,3,0,2:T(8,128)(2,1)}, u32[]{:S(2)}) copy-start(bf16[16,16,2,2,320]{4,1,3,0,2:T(8,128)(2,1)} %copy-done.10) | copy-start | bytes 1966084
  404.3 137.2 %all-reduce.7.cloned.1.call-start = ((), (), s32[]{:S(2)}) async-start(), calls=%async_computation.12 | async-start | bytes 409600
  449.5 5.6 copy-start.12
  449.5 5.6 copy-start.14
  449.5 173.2 %reduce-scatter.14.cloned.1.call-start = ((), (), s32[]{:S(2)}) async-start(), calls=%async_computation.11 | async-start | bytes 696320
  455.1 1.0 copy-start.15
  461.0 1.0 copy-start.15
  466.9 1.0 copy-start.15
  472.9 1.0 copy-start.15
  478.9 5.1 copy-start.9
  484.0 4.1 copy-start.23
  484.0 4.1 copy-start.24
  484.0 140.4 %copy-start.1 = (bf16[2,1280,320]{1,2,0:T(8,128)(2,1)S(1)}, bf16[2,1280,320]{1,2,0:T(8,128)(2,1)}, u32[]{:S(2)}) copy-start(bf16[2,1280,320]{1,2,0:T(8,128)(2,1)} %param.20) | copy-start | bytes 4915204
Sparse Core Ops, SparseCore 0:
  11.7 46.2 all-gather.6
  76.4 63.3 reduce-scatter.11
  159.6 36.8 all-gather.10
  198.8 38.9 all-gather.12
  249.2 123.9 all-reduce.8
  404.4 40.8 all-gather.8
  449.6 91.7 all-reduce.6
  545.4 77.3 reduce-scatter.13
where the time goes:
time: 633 us; the launch traced here: 631 us
  waiting for transfers between devices  463 us (73%)
  matrix products  78.8 us (12%)
  blocking collectives  25.4 us (4%)
  local copies, waits for them, and re-layouts  22.2 us (4%)
  between operations  15.2 us (2%)
  starting transfers between devices  13.1 us (2%)
  other arithmetic  13 us (2%)
    unnamed x11, waiting for transfers between devices  256 us
    reduce_scatter x1, waiting for transfers between devices, shards(): lax.psum_scatter(jnp.einsum('hsk,hkd->sd', context, proj_weight, preferre...  62.2 us
    all_gather x1, waiting for transfers between devices, shards(): full_norm = lax.all_gather(normed, 'tensor', axis=0, tiled=True)  46.4 us
    all_gather x1, waiting for transfers between devices, shards(): lax.all_gather(grad_landed[None], 'tensor', axis=0, tiled=True)  36.6 us
    all_gather x1, waiting for transfers between devices, shards(): full_grad = lax.all_gather(grad_mid, 'tensor', axis=0, tiled=True)  35.1 us
    all_gather x1, waiting for transfers between devices, shards(): arrived = lax.all_gather(landed[None], 'tensor', axis=0, tiled=True)  19 us
    all_to_all x1, blocking collectives, shards(): lax.all_to_all(outgoing, 'dp', split_axis=0, concat_axis=0, tiled=True)  13.8 us
  transfers between devices with their start and end apart: 10, of which 10 were waited for; matrix products, arithmetic and copies ran while one was open for 10% of the time, Pallas kernels for 0%

commit v1 on v0

--- a/solution.py
+++ b/solution.py
@@ -130,7 +130,16 @@
     places = group_count * local_experts * CAP
     normal_in, factor_in = norm_parts(tokens)
     normed = normal_in.astype(jnp.bfloat16)
-    full_norm = lax.all_gather(normed, "tensor", axis=0, tiled=True)
+    ways = lax.axis_size("tensor")
+    up = [(d, (d + 1) % ways) for d in range(ways)]
+    down = [(d, (d - 1) % ways) for d in range(ways)]
+    earlier, later = ([normed], [normed])
+    for _ in range(ways // 2):
+        earlier.append(lax.ppermute(earlier[-1], "tensor", up))
+    for _ in range((ways - 1) // 2):
+        later.append(lax.ppermute(later[-1], "tensor", down))
+    line = jnp.concatenate([*earlier[::-1], *later[1:]], axis=0)
+    full_norm = jnp.roll(line, (lax.axis_index("tensor") - ways // 2) * normed.shape[0], axis=0)
     seq_len = full_norm.shape[0]
     block_rows = min(512, seq_len)
     qkv_rows = jnp.einsum(

time: 633 us -> 664 us (1.049)
  starting transfers between devices: 13.1 us -> 34.2 us
  waiting for transfers between devices: 463 us -> 444 us
  local copies, waits for them, and re-layouts: 22.2 us -> 38.3 us
  matrix products: 78.8 us -> 91.6 us
    all_gather x1 -> x0, waiting for transfers between devices: 46.4 us -> none  [shards(): full_norm = lax.all_gather(normed, 'tensor', axis=0, tiled=True)]
    ppermute x0 -> x15, waiting for transfers between devices: none -> 42.5 us  [the longest x8 41.1 us: shards(): earlier.append(lax.ppermute(earlier[-1], 'tensor', up))]
    unnamed x11 -> x10, waiting for transfers between devices: 256 us -> 233 us
    ppermute x0 -> x15, starting transfers between devices: none -> 21.1 us  [the longest x7 21.1 us: shards(): later.append(lax.ppermute(later[-1], 'tensor', down))]
    unnamed x55 -> x102, local copies, waits for them, and re-layouts: 8.34 us -> 22.1 us
    dot_general x4, matrix products: 3.8 us -> 11.8 us  [head_one_block(): jnp.einsum('qt,qk->tk', shares.astype(jnp.bfloat16), grad_block, preferre...]
  transfers between devices with their start and end apart: 10 -> 24, of which waited for: 10 -> 19; matrix products, arithmetic and copies ran while one was open for 10% -> 13% of each run, Pallas kernels for 0% -> 0%
where the time goes in v1:
time: 664 us; the launch traced here: 662 us
  waiting for transfers between devices  444 us (67%)
  matrix products  91.6 us (14%)
  local copies, waits for them, and re-layouts  38.3 us (6%)
  starting transfers between devices  34.2 us (5%)
  blocking collectives  25 us (4%)
  between operations  15.5 us (2%)
  other arithmetic  13.1 us (2%)
    unnamed x10, waiting for transfers between devices  233 us
    reduce_scatter x1, waiting for transfers between devices, shards(): lax.psum_scatter(jnp.einsum('hsk,hkd->sd', context, proj_weight, preferre...  64.9 us
    ppermute x8, waiting for transfers between devices, shards(): earlier.append(lax.ppermute(earlier[-1], 'tensor', up))  41.1 us
    all_gather x1, waiting for transfers between devices, shards(): lax.all_gather(grad_landed[None], 'tensor', axis=0, tiled=True)  36.7 us
    all_gather x1, waiting for transfers between devices, shards(): full_grad = lax.all_gather(grad_mid, 'tensor', axis=0, tiled=True)  35.7 us
    unnamed x102, local copies, waits for them, and re-layouts  22.1 us
    ppermute x7, starting transfers between devices, shards(): later.append(lax.ppermute(later[-1], 'tensor', down))  21.1 us
    all_gather x1, waiting for transfers between devices, shards(): arrived = lax.all_gather(landed[None], 'tensor', axis=0, tiled=True)  20.4 us
  transfers between devices with their start and end apart: 24, of which 19 were waited for; matrix products, arithmetic and copies ran while one was open for 13% of the time, Pallas kernels for 0%

profile of v1, /device:TPU:2, one launch (start us, length us, event | category | flops | bytes accessed | tf_op | source)
XLA Modules:
  0.0 661.8 jit_solution(13883709570388416000)
XLA Ops:
  10.9 10.0 %collective-permute-done = bf16[128,1280]{1,0:T(8,128)(2,1)S(1)} collective-permute-done((bf16[128,1280]{1,0:T(8,128)(2,1)S(1)}, bf16[128,1280]{1,0:T(8,128)(2,1)S(1)}, u32[]{:S(2)}, u32[]{:S(2)}) %collective-permute-start) | collective-permute-done | bytes 327712 | tf_op jit(solution)/shard_map/ppermute | solution.py:138
  21.0 3.0 collective-permute-start.8
  23.9 4.8 collective-permute-done.1
  28.7 3.0 collective-permute-start.9
  31.7 4.7 collective-permute-done.2
  36.4 3.0 collective-permute-start.10
  39.4 4.7 collective-permute-done.3
  44.2 2.9 collective-permute-start.11
  47.1 4.7 collective-permute-done.4
  52.6 2.9 collective-permute-start.12
  55.5 4.0 collective-permute-done.5
  60.1 3.2 collective-permute-start.13
  63.3 4.0 collective-permute-done.6
  68.3 3.1 collective-permute-start.14
  71.4 4.0 collective-permute-done.7
  88.6 1.6 fusion.57
  90.2 2.4 copy-done.32
  96.0 8.1 %while.25 = (s32[]{:T(128)}, bf16[4,1,512,80]{2,3,1,0:T(8,128)(2,1)S(1)}, bf16[4,1,512,80]{3,2,1,0:T(8,128)(2,1)S(1)}, bf16[1,2048,80]{2,1,0:T(8,128)(2,1)S(1)}, bf16[1,2048,80]{2,1,0:T(8,128)(2,1)}, /*index=5*/s32[]{:T(128)}) while((s32[]{:T(128)}, bf16[4,1,512,80]{2,3,1,0:T(8,128)(2,1)S(1)}, bf16[4,1,512,80]{3,2,1,0:T(8,128)(2,1)S(1)}, ...), condition=%wide.region_4.5_spmd, body=%wide.region_2.4_spmd.sunk | while | flops 340827648 | bytes 10965097 | solution.py:57
  105.2 4.8 convolution_convert_fusion.1
  110.6 64.9 %reduce-scatter.12.cloned.1.call-done = bf16[128,1280]{1,0:T(8,128)(2,1)} async-done(((bf16[2048,1280]{1,0:T(8,128)(2,1)}), bf16[128,1280]{1,0:T(8,128)(2,1)}) %reduce-scatter.12.cloned.1.call-update) | async-done | bytes 327696 | tf_op jit(solution)/shard_map/reduce_scatter | solution.py:154
  177.3 13.5 %all_to_all.20 = bf16[16,2,2,1280]{3,2,1,0:T(2,128)(2,1)S(1)} all-to-all(bf16[16,2,2,1280]{3,2,1,0:T(2,128)(2,1)S(1)} %reshape.172), channel_id=1, replica_groups=mesh['dp'=16,'tensor'=16] {'dp'}, dimensions={0} | all-to-all | bytes 327680 | tf_op jit(solution)/shard_map/all_to_all | solution.py:175
  192.9 1.9 fusion.60
  195.8 11.4 %all_to_all.21 = bf16[16,2,2,1280]{3,2,1,0:T(2,128)(2,1)S(1)} all-to-all(bf16[16,2,2,1280]{3,2,1,0:T(2,128)(2,1)S(1)} %reshape.174), channel_id=1, replica_groups=mesh['dp'=16,'tensor'=16] {'dp'}, dimensions={0} | all-to-all | bytes 327680 | tf_op jit(solution)/shard_map/all_to_all | solution.py:202
  208.2 20.4 %all-gather.8.cloned.1.call-done = bf16[256,2,2,1280]{3,0,2,1:T(8,128)(2,1)} async-done(((bf16[16,2,2,1280]{3,0,2,1:T(8,128)(2,1)}), bf16[256,2,2,1280]{3,0,2,1:T(8,128)(2,1)}) %all-gather.8.cloned.1.call-update) | async-done | bytes 2621456 | tf_op jit(solution)/shard_map/all_gather | solution.py:176
  228.6 4.7 fusion.74
  233.3 36.7 %all-gather.10.cloned.1.call-done = bf16[256,2,2,1280]{3,0,2,1:T(8,128)(2,1)} async-done(((bf16[16,2,2,1280]{3,0,2,1:T(8,128)(2,1)}), bf16[256,2,2,1280]{3,0,2,1:T(8,128)(2,1)}) %all-gather.10.cloned.1.call-update) | async-done | bytes 2621456 | tf_op jit(solution)/shard_map/all_gather | solution.py:203
  270.0 4.3 fusion.72
  275.2 3.1 fusion.42
  278.3 3.1 fusion.41
  282.0 123.5 %all-reduce.9.cloned.1.call-done = (bf16[16,16,2,2,1280]{4,1,3,0,2:T(8,128)(2,1)}, bf16[16,16,2,2,1280]{4,1,3,0,2:T(8,128)(2,1)}) async-done(((bf16[16,16,2,2,1280]{4,1,3,0,2:T(8,128)(2,1)}, bf16[16,16,2,2,1280]{4,1,3,0,2:T(8,128)(2,1)}), (bf16[16,16,2,2,1280]{4,1,3,0,2:T(8,128)(2,1)}, bf16[16,16,2,2,1280]{4,1,3,0,2:T(8,128)(2,1)})) %all-reduce.9.cloned.1.call-update) | async-done | bytes 5242896
  405.5 1.6 dynamic-slice_bitcast_fusion
  407.8 7.3 %all-to-all-start.3 = ((bf16[16,2,2,1280]{3,2,1,0:T(2,128)(2,1)}), bf16[16,2,2,1280]{3,2,1,0:T(2,128)(2,1)S(1)}, u32[]{:S(2)}, u32[]{:S(2)}) async-start(bf16[16,2,2,1280]{3,2,1,0:T(2,128)(2,1)} %copy.57), calls=%async_computation.4 | async-start | bytes 327680 | tf_op jit(solution)/shard_map/all_to_all | solution.py:106
  415.1 1.6 dynamic-slice_bitcast_fusion.1
  417.5 4.1 all-to-all-done.3
  421.6 5.1 all-to-all-start.1
  427.2 6.0 all-to-all-done.1
  436.3 4.0 fusion.44
  440.3 35.7 %all-gather.6.cloned.1.call-done = bf16[2048,1280]{1,0:T(8,128)(2,1)} async-done(((bf16[128,1280]{1,0:T(8,128)(2,1)}), bf16[2048,1280]{1,0:T(8,128)(2,1)}) %all-gather.6.cloned.1.call-update) | async-done | bytes 5242896 | tf_op jit(solution)/shard_map/all_gather | solution.py:222
  476.0 4.2 fusion.62
  480.5 4.2 fusion.61
  485.7 44.4 %while.26 = (s32[]{:T(128)}, f32[1,2048,80]{1,2,0:T(8,128)S(1)}, f32[1,2048,80]{1,2,0:T(8,128)}, bf16[4,1,512,80]{2,3,1,0:T(8,128)(2,1)}, bf16[4,1,512,80]{3,2,1...) while((s32[]{:T(128)}, f32[1,2048,80]{1,2,0:T(8,128)S(1)}, ...), condition=%wide.region_17.18_spmd.clone, body=%wide.region_14.17_spmd.clone.sunk | while | flops 855284736 | bytes 73365768 | solution.py:92
  485.7 1.9 fusion.164
  487.6 1.4 multiply_reduce_fusion.2
  490.8 1.6 fusion.165
  492.4 1.4 fusion.167
  493.8 2.8 fusion.166
  496.6 1.9 fusion.164
  498.5 1.4 multiply_reduce_fusion.2
  501.7 1.6 fusion.165
  503.3 1.4 fusion.167
  504.7 3.0 fusion.166
  507.7 1.9 fusion.164
  512.8 1.6 fusion.165
  514.5 1.4 fusion.167
  515.9 3.0 fusion.166
  518.9 1.9 fusion.164
  524.0 1.6 fusion.165
  525.6 1.4 fusion.167
  527.0 3.0 fusion.166
  532.2 4.0 fusion.54
  537.4 4.1 fusion.43
  542.1 30.0 %all-reduce.7.cloned.1.call-done = bf16[1,80,1280]{2,1,0:T(8,128)(2,1)} async-done(((bf16[1,80,1280]{2,1,0:T(8,128)(2,1)}), bf16[1,80,1280]{2,1,0:T(8,128)(2,1)}) %all-reduce.7.cloned.1.call-update) | async-done | bytes 204816
  572.1 1.5 dynamic-slice_convert_fusion
  573.5 79.8 %reduce-scatter.14.cloned.1.call-done = bf16[80,240]{1,0:T(8,128)(2,1)} async-done(((bf16[1280,240]{1,0:T(8,128)(2,1)}), bf16[80,240]{1,0:T(8,128)(2,1)}) %reduce-scatter.14.cloned.1.call-update) | async-done | bytes 38416
  (235 shorter events, 60.1 us)
Async XLA Ops:
  7.2 221.4 %copy-start = (bf16[2,1280,320]{1,2,0:T(8,128)(2,1)S(1)}, bf16[2,1280,320]{1,2,0:T(8,128)(2,1)}, u32[]{:S(2)}) copy-start(bf16[2,1280,320]{1,2,0:T(8,128)(2,1)} %param.20) | copy-start | bytes 4915204
  7.2 74.4 %copy-start.5 = (bf16[128,1280]{1,0:T(8,128)(2,1)S(1)}, bf16[128,1280]{1,0:T(8,128)(2,1)}, u32[]{:S(2)}) copy-start(bf16[128,1280]{1,0:T(8,128)(2,1)} %param.13) | copy-start | bytes 983044
  7.2 168.4 %reduce-scatter.12.cloned.1.call-start = ((), (), s32[]{:S(2)}) async-start(), calls=%async_computation.6 | async-start | bytes 5570560 | tf_op jit(solution)/shard_map/reduce_scatter | solution.py:154
  10.9 10.1 %collective-permute-start = (bf16[128,1280]{1,0:T(8,128)(2,1)S(1)}, bf16[128,1280]{1,0:T(8,128)(2,1)S(1)}, u32[]{:S(2)}, u32[]{:S(2)}) collective-permute-start(bf16[128,1280]{1,0:T(8,128)(2,1)S(1)} %fusion.99), channel_id=1, source_target_pairs={{0,1},{1,2},{2,3},{3,4},{4,5},{5,6},{6,7},{7,8},{8,9},{9,10},{10,1... | collective-permute-start | bytes 983048 | tf_op jit(solution)/shard_map/ppermute | solution.py:138
  21.0 7.7 %collective-permute-start.1 = (bf16[128,1280]{1,0:T(8,128)(2,1)S(1)}, bf16[128,1280]{1,0:T(8,128)(2,1)S(1)}, u32[]{:S(2)}, u32[]{:S(2)}) collective-permute-start(bf16[128,1280]{1,0:T(8,128)(2,1)S(1)} %collective-permute-done), channel_id=1, source_target_pairs={{0,1},{1,2},{2,3},{3,4},{4,5},{5,6},{6,7},{7,8},{8,9},{9,10},{10,1... | collective-permute-start | bytes 983048 | tf_op jit(solution)/shard_map/ppermute | solution.py:138
  21.0 7.7 %collective-permute-start.8 = (bf16[128,1280]{1,0:T(8,128)(2,1)S(1)}, bf16[128,1280]{1,0:T(8,128)(2,1)S(1)}, u32[]{:S(2)}, u32[]{:S(2)}) collective-permute-start(bf16[128,1280]{1,0:T(8,128)(2,1)S(1)} %fusion.99), channel_id=1, source_target_pairs={{0,15},{1,0},{2,1},{3,2},{4,3},{5,4},{6,5},{7,6},{8,7},{9,8},{10,9... | collective-permute-start | bytes 983048 | tf_op jit(solution)/shard_map/ppermute | solution.py:140
  28.7 7.7 %collective-permute-start.2 = (bf16[128,1280]{1,0:T(8,128)(2,1)S(1)}, bf16[128,1280]{1,0:T(8,128)(2,1)S(1)}, u32[]{:S(2)}, u32[]{:S(2)}) collective-permute-start(bf16[128,1280]{1,0:T(8,128)(2,1)S(1)} %collective-permute-done.1), channel_id=1, source_target_pairs={{0,1},{1,2},{2,3},{3,4},{4,5},{5,6},{6,7},{7,8},{8,9},{9,10},{10,1... | collective-permute-start | bytes 983048 | tf_op jit(solution)/shard_map/ppermute | solution.py:138
  28.7 7.7 %collective-permute-start.9 = (bf16[128,1280]{1,0:T(8,128)(2,1)S(1)}, bf16[128,1280]{1,0:T(8,128)(2,1)S(1)}, u32[]{:S(2)}, u32[]{:S(2)}) collective-permute-start(bf16[128,1280]{1,0:T(8,128)(2,1)S(1)} %collective-permute-done.8), channel_id=1, source_target_pairs={{0,15},{1,0},{2,1},{3,2},{4,3},{5,4},{6,5},{7,6},{8,7},{9,8},{10,9... | collective-permute-start | bytes 983048 | tf_op jit(solution)/shard_map/ppermute | solution.py:140
  36.4 7.7 %copy-start.10 = (bf16[128,1280]{1,0:T(8,128)(2,1)}, bf16[128,1280]{1,0:T(8,128)(2,1)S(1)}, u32[]{:S(2)}) copy-start(bf16[128,1280]{1,0:T(8,128)(2,1)S(1)} %collective-permute-done.2) | copy-start | bytes 983044
  36.4 7.7 %collective-permute-start.3 = (bf16[128,1280]{1,0:T(8,128)(2,1)S(1)}, bf16[128,1280]{1,0:T(8,128)(2,1)S(1)}, u32[]{:S(2)}, u32[]{:S(2)}) collective-permute-start(bf16[128,1280]{1,0:T(8,128)(2,1)S(1)} %collective-permute-done.2), channel_id=1, source_target_pairs={{0,1},{1,2},{2,3},{3,4},{4,5},{5,6},{6,7},{7,8},{8,9},{9,10},{10,1... | collective-permute-start | bytes 983048 | tf_op jit(solution)/shard_map/ppermute | solution.py:138
  36.4 7.7 %collective-permute-start.10 = (bf16[128,1280]{1,0:T(8,128)(2,1)S(1)}, bf16[128,1280]{1,0:T(8,128)(2,1)S(1)}, u32[]{:S(2)}, u32[]{:S(2)}) collective-permute-start(bf16[128,1280]{1,0:T(8,128)(2,1)S(1)} %collective-permute-done.9), channel_id=1, source_target_pairs={{0,15},{1,0},{2,1},{3,2},{4,3},{5,4},{6,5},{7,6},{8,7},{9,8},{10,9... | collective-permute-start | bytes 983048 | tf_op jit(solution)/shard_map/ppermute | solution.py:140
  44.1 16.0 %copy-start.16 = (bf16[128,1280]{1,0:T(8,128)(2,1)}, bf16[128,1280]{1,0:T(8,128)(2,1)S(1)}, u32[]{:S(2)}) copy-start(bf16[128,1280]{1,0:T(8,128)(2,1)S(1)} %collective-permute-done.3) | copy-start | bytes 983044
  44.1 7.7 %collective-permute-start.4 = (bf16[128,1280]{1,0:T(8,128)(2,1)S(1)}, bf16[128,1280]{1,0:T(8,128)(2,1)S(1)}, u32[]{:S(2)}, u32[]{:S(2)}) collective-permute-start(bf16[128,1280]{1,0:T(8,128)(2,1)S(1)} %collective-permute-done.3), channel_id=1, source_target_pairs={{0,1},{1,2},{2,3},{3,4},{4,5},{5,6},{6,7},{7,8},{8,9},{9,10},{10,1... | collective-permute-start | bytes 983048 | tf_op jit(solution)/shard_map/ppermute | solution.py:138
  44.2 7.7 %collective-permute-start.11 = (bf16[128,1280]{1,0:T(8,128)(2,1)S(1)}, bf16[128,1280]{1,0:T(8,128)(2,1)S(1)}, u32[]{:S(2)}, u32[]{:S(2)}) collective-permute-start(bf16[128,1280]{1,0:T(8,128)(2,1)S(1)} %collective-permute-done.10), channel_id=1, source_target_pairs={{0,15},{1,0},{2,1},{3,2},{4,3},{5,4},{6,5},{7,6},{8,7},{9,8},{10,9... | collective-permute-start | bytes 983048 | tf_op jit(solution)/shard_map/ppermute | solution.py:140
  51.8 11.5 %copy-start.18 = (bf16[128,1280]{1,0:T(8,128)(2,1)}, bf16[128,1280]{1,0:T(8,128)(2,1)S(1)}, u32[]{:S(2)}) copy-start(bf16[128,1280]{1,0:T(8,128)(2,1)S(1)} %collective-permute-done.4) | copy-start | bytes 983044
  51.8 7.7 %collective-permute-start.5 = (bf16[128,1280]{1,0:T(8,128)(2,1)S(1)}, bf16[128,1280]{1,0:T(8,128)(2,1)S(1)}, u32[]{:S(2)}, u32[]{:S(2)}) collective-permute-start(bf16[128,1280]{1,0:T(8,128)(2,1)S(1)} %collective-permute-done.4), channel_id=1, source_target_pairs={{0,1},{1,2},{2,3},{3,4},{4,5},{5,6},{6,7},{7,8},{8,9},{9,10},{10,1... | collective-permute-start | bytes 983048 | tf_op jit(solution)/shard_map/ppermute | solution.py:138
  52.6 7.5 %collective-permute-start.12 = (bf16[128,1280]{1,0:T(8,128)(2,1)S(1)}, bf16[128,1280]{1,0:T(8,128)(2,1)}, u32[]{:S(2)}, u32[]{:S(2)}) collective-permute-start(bf16[128,1280]{1,0:T(8,128)(2,1)S(1)} %collective-permute-done.11), channel_id=1, source_target_pairs={{0,15},{1,0},{2,1},{3,2},{4,3},{5,4},{6,5},{7,6},{8,7},{9,8},{10,9... | collective-permute-start | bytes 983048 | tf_op jit(solution)/shard_map/ppermute | solution.py:140
  59.5 7.8 %copy-start.20 = (bf16[128,1280]{1,0:T(8,128)(2,1)}, bf16[128,1280]{1,0:T(8,128)(2,1)S(1)}, u32[]{:S(2)}) copy-start(bf16[128,1280]{1,0:T(8,128)(2,1)S(1)} %collective-permute-done.5) | copy-start | bytes 983044
  59.5 7.8 %collective-permute-start.6 = (bf16[128,1280]{1,0:T(8,128)(2,1)S(1)}, bf16[128,1280]{1,0:T(8,128)(2,1)}, u32[]{:S(2)}, u32[]{:S(2)}) collective-permute-start(bf16[128,1280]{1,0:T(8,128)(2,1)S(1)} %collective-permute-done.5), channel_id=1, source_target_pairs={{0,1},{1,2},{2,3},{3,4},{4,5},{5,6},{6,7},{7,8},{8,9},{9,10},{10,1... | collective-permute-start | bytes 983048 | tf_op jit(solution)/shard_map/ppermute | solution.py:138
  60.1 8.1 %collective-permute-start.13 = (bf16[128,1280]{1,0:T(8,128)(2,1)}, bf16[128,1280]{1,0:T(8,128)(2,1)}, u32[]{:S(2)}, u32[]{:S(2)}) collective-permute-start(bf16[128,1280]{1,0:T(8,128)(2,1)} %collective-permute-done.12), channel_id=1, source_target_pairs={{0,15},{1,0},{2,1},{3,2},{4,3},{5,4},{6,5},{7,6},{8,7},{9,8},{10,9... | collective-permute-start | bytes 983048 | tf_op jit(solution)/shard_map/ppermute | solution.py:140
  67.4 8.0 %collective-permute-start.7 = (bf16[128,1280]{1,0:T(8,128)(2,1)}, bf16[128,1280]{1,0:T(8,128)(2,1)}, u32[]{:S(2)}, u32[]{:S(2)}) collective-permute-start(bf16[128,1280]{1,0:T(8,128)(2,1)} %collective-permute-done.6), channel_id=1, source_target_pairs={{0,1},{1,2},{2,3},{3,4},{4,5},{5,6},{6,7},{7,8},{8,9},{9,10},{10,1... | collective-permute-start | bytes 983048 | tf_op jit(solution)/shard_map/ppermute | solution.py:138
  67.4 14.5 %copy-start.13 = (bf16[128,1280]{1,0:T(8,128)(2,1)S(1)}, bf16[128,1280]{1,0:T(8,128)(2,1)}, u32[]{:S(2)}) copy-start(bf16[128,1280]{1,0:T(8,128)(2,1)} %copy-done.12) | copy-start | bytes 983044
  67.4 14.5 %copy-start.15 = (bf16[128,1280]{1,0:T(8,128)(2,1)S(1)}, bf16[128,1280]{1,0:T(8,128)(2,1)}, u32[]{:S(2)}) copy-start(bf16[128,1280]{1,0:T(8,128)(2,1)} %copy-done.14) | copy-start | bytes 983044
  68.3 15.7 %collective-permute-start.14 = (bf16[128,1280]{1,0:T(8,128)(2,1)}, bf16[128,1280]{1,0:T(8,128)(2,1)S(1)}, u32[]{:S(2)}, u32[]{:S(2)}) collective-permute-start(bf16[128,1280]{1,0:T(8,128)(2,1)} %collective-permute-done.13), channel_id=1, source_target_pairs={{0,15},{1,0},{2,1},{3,2},{4,3},{5,4},{6,5},{7,6},{8,7},{9,8},{10,9... | collective-permute-start | bytes 983048 | tf_op jit(solution)/shard_map/ppermute | solution.py:140
  80.4 5.6 copy-start.21
  81.4 4.6 copy-start.19
  81.5 4.6 copy-start.17
  81.5 4.6 copy-start.11
  88.6 4.0 copy-start.32
  104.1 129.2 %copy-start.4 = (bf16[4,1,512,80]{3,2,1,0:T(8,128)(2,1)}, bf16[4,1,512,80]{3,2,1,0:T(8,128)(2,1)S(1)}, u32[]{:S(2)}) copy-start(bf16[4,1,512,80]{3,2,1,0:T(8,128)(2,1)S(1)} %get-tuple-element.373) | copy-start | bytes 983044
  109.9 81.7 %copy-start.35 = (f32[128,2]{0,1:T(2,128)S(1)}, f32[128,2]{0,1:T(2,128)}, u32[]{:S(2)}) copy-start(f32[128,2]{0,1:T(2,128)} %param.15) | copy-start | bytes 3076
  109.9 118.6 %all-gather.8.cloned.1.call-start = ((), (), s32[]{:S(2)}) async-start(), calls=%async_computation.8 | async-start | bytes 2785280 | tf_op jit(solution)/shard_map/all_gather | solution.py:176
  191.6 78.4 %all-gather.10.cloned.1.call-start = ((), (), s32[]{:S(2)}) async-start(), calls=%async_computation.9 | async-start | bytes 2785280 | tf_op jit(solution)/shard_map/all_gather | solution.py:203
  207.9 197.5 %all-reduce.9.cloned.1.call-start = ((), (), s32[]{:S(2)}) async-start(), calls=%async_computation.12 | async-start | bytes 10485760
  275.2 3.1 copy-start.8
  275.2 3.1 copy-start.23
  278.3 3.1 copy-start.38
  281.3 152.3 %copy-start.9 = (bf16[128,1280]{1,0:T(8,128)(2,1)S(1)}, bf16[128,1280]{1,0:T(8,128)(2,1)}, u32[]{:S(2)}) copy-start(bf16[128,1280]{1,0:T(8,128)(2,1)} %param.14) | copy-start | bytes 983044
  281.4 153.7 %copy-start.37 = (u32[256]{0:T(256)S(1)}, u32[256]{0:T(256)}, u32[]{:S(2)}) copy-start(u32[256]{0:T(256)} %constant.106) | copy-start | bytes 3076
  281.4 154.9 %copy-start.26 = (bf16[16,16,2,2,320]{4,1,3,0,2:T(8,128)(2,1)S(1)}, bf16[16,16,2,2,320]{4,1,3,0,2:T(8,128)(2,1)}, u32[]{:S(2)}) copy-start(bf16[16,16,2,2,320]{4,1,3,0,2:T(8,128)(2,1)} %copy-done.25) | copy-start | bytes 1966084
  407.8 13.7 %all-to-all-start.3 = ((bf16[16,2,2,1280]{3,2,1,0:T(2,128)(2,1)}), bf16[16,2,2,1280]{3,2,1,0:T(2,128)(2,1)S(1)}, u32[]{:S(2)}, u32[]{:S(2)}) async-start(bf16[16,2,2,1280]{3,2,1,0:T(2,128)(2,1)} %copy.57), calls=%async_computation.4 | async-start | bytes 327680 | tf_op jit(solution)/shard_map/all_to_all | solution.py:106
  421.6 11.6 %all-to-all-start.1 = ((bf16[16,2,2,1280]{3,2,1,0:T(2,128)(2,1)}), bf16[16,2,2,1280]{3,2,1,0:T(2,128)(2,1)S(1)}, u32[]{:S(2)}, u32[]{:S(2)}) async-start(bf16[16,2,2,1280]{3,2,1,0:T(2,128)(2,1)} %copy.54), calls=%async_computation.2 | async-start | bytes 327680 | tf_op jit(solution)/shard_map/all_to_all | solution.py:106
  426.7 49.2 %all-gather.6.cloned.1.call-start = ((), (), s32[]{:S(2)}) async-start(), calls=%async_computation.7 | async-start | bytes 5570560 | tf_op jit(solution)/shard_map/all_gather | solution.py:222
  433.6 42.4 %copy-start.7 = (bf16[10,8,4,512]{3,1,2,0:T(8,128)(2,1)S(1)}, bf16[10,8,4,512]{3,1,2,0:T(8,128)(2,1)}, u32[]{:S(2)}) copy-start(bf16[10,8,4,512]{3,1,2,0:T(8,128)(2,1)} %copy-done.6) | copy-start | bytes 983044
  435.0 137.1 %all-reduce.7.cloned.1.call-start = ((), (), s32[]{:S(2)}) async-start(), calls=%async_computation.11 | async-start | bytes 409600
  440.3 40.2 %copy-start.22 = (bf16[1,80,1280]{2,1,0:T(8,128)(2,1)S(1)}, bf16[1,80,1280]{2,1,0:T(8,128)(2,1)}, u32[]{:S(2)}) copy-start(bf16[1,80,1280]{2,1,0:T(8,128)(2,1)} %param.19) | copy-start | bytes 614404
  480.2 5.5 copy-start.28
  480.2 173.1 %reduce-scatter.14.cloned.1.call-start = ((), (), s32[]{:S(2)}) async-start(), calls=%async_computation.10 | async-start | bytes 696320
  485.7 3.3 copy-start.30
  490.7 3.1 copy-start.3
  496.6 3.3 copy-start.30
  501.7 3.1 copy-start.3
  504.7 3.0 copy-start.29
  504.7 3.0 copy-start.31
  507.7 3.3 copy-start.30
  512.8 3.1 copy-start.3
  515.9 3.0 copy-start.29
  515.9 3.0 copy-start.31
  518.9 3.3 copy-start.30
  524.0 3.1 copy-start.3
  527.0 3.0 copy-start.29
  527.0 3.0 copy-start.31
  532.2 5.2 copy-start.24
  537.4 117.6 %copy-start.1 = (bf16[2,1280,320]{1,2,0:T(8,128)(2,1)S(1)}, bf16[2,1280,320]{1,2,0:T(8,128)(2,1)}, u32[]{:S(2)}) copy-start(bf16[2,1280,320]{1,2,0:T(8,128)(2,1)} %param.20) | copy-start | bytes 4915204
  (17 other events, 27.2 us)
Sparse Core Ops, SparseCore 0:
  110.1 65.4 reduce-scatter.11
  191.7 36.8 all-gather.7
  231.0 38.9 all-gather.9
  281.5 123.9 all-reduce.8
  435.1 40.8 all-gather.5
  480.3 91.7 all-reduce.6
  575.9 77.3 reduce-scatter.13
